TPU v7x, 32 devices: a whole 2x2x4 slice. The times are simulated.
32 devices in a mesh: band: 4 (over y, core), shard: 8 (over z, x).
Axes of the slice: x: 2, y: 2, z: 4, core: 2. Of those that a mesh axis runs over, the one named last changes fastest.
Arguments:
- block_input: bfloat16 [8, 56, 14, 512], P('shard', 'band'), may hold values from -6 to 6
- output_grad: bfloat16 [8, 56, 14, 512], P('shard', 'band'), may hold values from -6 to 6
- region_ids: int32 [56, 14], P('band'), may hold values from 0 to 8, as said below
- relative_index: int32 [49, 49], replicated, may hold values from 0 to 168
- attention_weight: float32 [512, 2048], P('shard'), may hold values from -0.375 to 0.375
- expand_weight: float32 [512, 2048], P('shard'), may hold values from -0.25 to 0.25
- reduce_weight: float32 [2048, 512], P('shard'), may hold values from -0.125 to 0.125
- vectors: float32 [12, 512], P(None, 'shard'), may hold values from -0.5 to 0.5
- bias_table: float32 [169, 16], replicated, may hold values from -0.6 to 250
- attention_mean: float32 [512, 2048], P('shard'), may hold values from -0.3 to 0.3
- attention_square: float32 [512, 2048], P('shard'), may hold values from 0.0001 to 0.001
- expand_mean: float32 [512, 2048], P('shard'), may hold values from -0.3 to 0.3
- expand_square: float32 [512, 2048], P('shard'), may hold values from 0.0001 to 0.001
- reduce_mean: float32 [2048, 512], P('shard'), may hold values from -0.3 to 0.3
- reduce_square: float32 [2048, 512], P('shard'), may hold values from 0.0001 to 0.001
- vectors_mean: float32 [12, 512], P(None, 'shard'), may hold values from -0.3 to 0.3
- vectors_square: float32 [12, 512], P(None, 'shard'), may hold values from 0.0001 to 0.001
- table_mean: float32 [169, 16], replicated, may hold values from -0.3 to 0.3
- table_square: float32 [169, 16], replicated, may hold values from 0.0001 to 0.001
Outputs:
- block_output: float32 [8, 56, 14, 512], P('shard', 'band')
- input_grad: float32 [8, 56, 14, 512], P('shard', 'band')
- attention_grad: float32 [512, 2048], P('shard')
- expand_grad: float32 [512, 2048], P('shard')
- reduce_grad: float32 [2048, 512], P('shard')
- vectors_grad: float32 [12, 512], P(None, 'shard')
- table_grad: float32 [169, 16], replicated
- new_attention: float32 [512, 2048], P('shard')
- new_expand: float32 [512, 2048], P('shard')
- new_reduce: float32 [2048, 512], P('shard')
- new_vectors: float32 [12, 512], P(None, 'shard')
- new_table: float32 [169, 16], replicated
- new_attention_mean: float32 [512, 2048], P('shard')
- new_attention_square: float32 [512, 2048], P('shard')
- new_expand_mean: float32 [512, 2048], P('shard')
- new_expand_square: float32 [512, 2048], P('shard')
- new_reduce_mean: float32 [2048, 512], P('shard')
- new_reduce_square: float32 [2048, 512], P('shard')
- new_vectors_mean: float32 [12, 512], P(None, 'shard')
- new_vectors_square: float32 [12, 512], P(None, 'shard')
- new_table_mean: float32 [169, 16], replicated
- new_table_square: float32 [169, 16], replicated
Inputs may be any that keep to these rules, and one draw needn't show every extreme that they name: region_ids[r, c] = 3 * a(r) + b(c), where a(r) is 0 for r < 49, 1 from there up to a cut inside the last 7 rows, 2 from the cut on; b(c) likewise over the 14 columns with a cut of its own; each cut leaves 1 to 6 tokens in region 2.
All inputs are finite; a program needn't handle non-finite values.
Results may differ from a plain program's by a relative error of at most 0.023.
Values may be sent and summed in bfloat16 or wider, within the bound.
A program may use at most 128 MiB of HBM per device.

v0:
```python
import math

import jax
import jax.numpy as jnp
from jax import lax
from jax.experimental import pallas as pl
from jax.experimental.pallas import tpu as pltpu
from jax.sharding import PartitionSpec as P

WIN = 7
SHIFT = 3
STEP = 5


NORM_EPS = 1e-05
LEARN_RATE = 0.02
BETA_ONE = 0.9
BETA_TWO = 0.999
ADAM_EPS = 1e-08
WEIGHT_DECAY = 0.05
MASK_VALUE = -1000000000.0


BF = jnp.bfloat16
F32 = jnp.float32
MESH_ID = pl.DeviceIdType.MESH


def ring_position(index, count):
    column, row = index % 2, index // 2
    return (1 - column) * row + column * (count - 1 - row)


def ring_index(position, count):
    back = position // (count // 2)
    return (1 - back) * (2 * position) + back * (2 * (count - 1 - position) + 1)


def remote(src, dst, send, recv, **where):
    return pltpu.make_async_remote_copy(
        src_ref=src, dst_ref=dst, send_sem=send, recv_sem=recv, device_id=where, device_id_type=MESH_ID
    )


def greet(places):
    barrier = pltpu.get_barrier_semaphore()
    for where in places:
        pl.semaphore_signal(barrier, inc=1, device_id=where, device_id_type=MESH_ID)
    pl.semaphore_wait(barrier, len(places))


def gather_kernel(
    count, att, exp, red, vec, out_att, out_exp, out_red, out_vec,
    ring_send, ring_recv, pair_send, pair_recv, vec_send, vec_recv, own_sem,
):
    shard = lax.axis_index("shard")
    band = lax.axis_index("band")
    core = band % 2
    partner = band + 1 - 2 * core
    pos = ring_position(shard, count)
    to_right = ring_index((pos + 1) % count, count)
    to_left = ring_index((pos + count - 1) % count, count)
    peers = [(shard + j) % count for j in range(1, count)]
    greet([{"shard": peer} for peer in peers] + [{"band": partner}])

    def parts(block, quarter):
        lanes = pl.ds(pl.multiple_of(quarter * 512, 512), 512)
        return (
            out_att.at[block, :, lanes],
            out_exp.at[block, :, lanes],
            out_red.at[block, quarter],
        )

    def own_parts(quarter):
        lanes = pl.ds(pl.multiple_of(quarter * 512, 512), 512)
        return (att.at[:, lanes], exp.at[:, lanes], red.at[quarter])

    sends = []

    def send_ring(way, step):
        quarter = 2 * core + way
        block = ring_index((pos - step + count) % count if way == 0 else (pos + step) % count, count)
        target = to_right if way == 0 else to_left
        sources = own_parts(quarter) if step == 0 else parts(block, quarter)
        for k, (source, place) in enumerate(zip(sources, parts(block, quarter))):
            copy = remote(source, place, ring_send.at[way, step, k], ring_recv.at[way, step, k], shard=target)
            copy.start()
            sends.append(copy)

    for way in range(2):
        send_ring(way, 0)
    own = [
        pltpu.make_async_copy(source, place, own_sem.at[k])
        for k, (source, place) in enumerate(
            ((att, out_att.at[shard]), (exp, out_exp.at[shard]), (red, out_red.at[shard]), (vec, out_vec.at[shard]))
        )
    ]
    for copy in own:
        copy.start()
    for peer, j in zip(peers, range(count - 1)):
        copy = remote(vec, out_vec.at[shard], vec_send.at[j], vec_recv.at[j], shard=peer)
        copy.start()
        sends.append(copy)
    for step in range(count - 1):
        for way in range(2):
            quarter = 2 * core + way
            block = ring_index(
                (pos - step - 1 + count) % count if way == 0 else (pos + step + 1) % count, count
            )
            places = parts(block, quarter)
            for k, place in enumerate(places):
                remote(
                    place, place, ring_send.at[way, step, k], ring_recv.at[way, step, k], shard=to_right
                ).wait_recv()
            if step < count - 2:
                send_ring(way, step + 1)
            for k, place in enumerate(places):
                copy = remote(place, place, pair_send.at[way, step, k], pair_recv.at[way, step, k], band=partner)
                copy.start()
                sends.append(copy)
    for step in range(count - 1):
        for way in range(2):
            quarter = 2 * (1 - core) + way
            block = ring_index(
                (pos - step - 1 + count) % count if way == 0 else (pos + step + 1) % count, count
            )
            for k, place in enumerate(parts(block, quarter)):
                remote(
                    place, place, pair_send.at[way, step, k], pair_recv.at[way, step, k], band=partner
                ).wait_recv()
    for j in range(count - 1):
        source = (shard + count - 1 - j) % count
        remote(vec, out_vec.at[source], vec_send.at[j], vec_recv.at[j], shard=source).wait_recv()
    for copy in sends:
        copy.wait_send()
    for copy in own:
        copy.wait()


VM = pl.BlockSpec(memory_space=pltpu.VMEM)


def gather_shards(att, exp, red, vec):
    count = lax.axis_size("shard")
    rows = att.shape[0]
    dma = pltpu.SemaphoreType.DMA
    return pl.pallas_call(
        lambda *refs: gather_kernel(count, *refs),
        out_shape=(
            jax.ShapeDtypeStruct((count, rows, att.shape[1]), BF),
            jax.ShapeDtypeStruct((count, rows, exp.shape[1]), BF),
            jax.ShapeDtypeStruct((count,) + red.shape, BF),
            jax.ShapeDtypeStruct((count,) + vec.shape, BF),
        ),
        in_specs=[VM] * 4,
        out_specs=[VM] * 4,
        scratch_shapes=[
            dma((2, count - 1, 3)), dma((2, count - 1, 3)), dma((2, count - 1, 3)), dma((2, count - 1, 3)),
            dma((count - 1,)), dma((count - 1,)), dma((4,)),
        ],
        compiler_params=pltpu.CompilerParams(
            collective_id=0, has_side_effects=True, vmem_limit_bytes=48 * 1024 * 1024
        ),
        name="gather_shards",
    )(att, exp, red, vec)


def reduce_kernel(
    count, bands, att, exp, red, small, out_att, out_exp, out_red, out_small,
    paired, sent, got, done, others, mixed, small_band, small_shard,
    pair_send, pair_recv, ring_send, ring_recv, far_send, far_recv, mix_send, mix_recv,
    sb_send, sb_recv, ss_send, ss_recv,
):
    shard = lax.axis_index("shard")
    band = lax.axis_index("band")
    core = band % 2
    partner = band + 1 - 2 * core
    pos = ring_position(shard, count)
    to_right = ring_index((pos + 1) % count, count)
    to_left = ring_index((pos + count - 1) % count, count)
    shard_peers = [(shard + j) % count for j in range(1, count)]
    band_peers = [(band + j) % bands for j in range(1, bands)]
    rows = att.shape[1]
    greet([{"shard": peer} for peer in shard_peers] + [{"band": peer} for peer in band_peers])

    def block_of(way, step):
        if way == 0:
            return ring_index((pos - 1 - step + 2 * count) % count, count)
        return ring_index((pos + 1 + step) % count, count)

    def own_parts(block, quarter):
        lanes = pl.ds(pl.multiple_of(quarter * 512, 512), 512)
        return (att.at[block, :, lanes], exp.at[block, :, lanes], red.at[block, quarter])

    waits = []

    def pair_copy(way, step, k):
        block = block_of(way, step)
        source = own_parts(block, 2 * (1 - core) + way)[k]
        return remote(
            source, paired.at[way, step, k], pair_send.at[way, step, k], pair_recv.at[way, step, k], band=partner
        )

    for step in range(count):
        for way in range(2):
            for k in range(3):
                copy = pair_copy(way, step, k)
                copy.start()
                waits.append(copy)
        if step == 0:
            small_band[band] = small[...]
            for j, peer in enumerate(band_peers):
                copy = remote(small, small_band.at[band], sb_send.at[j], sb_recv.at[j], band=peer)
                copy.start()
                waits.append(copy)

    for step in range(count):
        for way in range(2):
            block = block_of(way, step)
            quarter = 2 * core + way
            if step > 0:
                remote(
                    sent.at[way, step - 1], got.at[way, step - 1],
                    ring_send.at[way, step - 1], ring_recv.at[way, step - 1], shard=to_right,
                ).wait_recv()
            lanes = pl.ds(pl.multiple_of(quarter * 512, 512), 512)
            for k in range(3):
                pair_copy(way, step, k).wait_recv()
                mine = (
                    att[block, :, lanes] if k == 0 else exp[block, :, lanes] if k == 1 else red[block, quarter]
                )
                total = mine.astype(F32) + paired[way, step, k].astype(F32)
                if step > 0:
                    total = total + got[way, step - 1, k].astype(F32)
                if step < count - 1:
                    sent[way, step, k] = total.astype(BF)
                else:
                    done[way, k] = total.astype(BF)
            if step < count - 1:
                copy = remote(
                    sent.at[way, step], got.at[way, step], ring_send.at[way, step], ring_recv.at[way, step],
                    shard=to_right if way == 0 else to_left,
                )
            else:
                for j in range(1, bands // 2):
                    copy = remote(
                        done.at[way], others.at[j - 1, way], far_send.at[j - 1, way], far_recv.at[j - 1, way],
                        band=(band + 2 * j) % bands,
                    )
                    copy.start()
                    waits.append(copy)
                continue
            copy.start()
            waits.append(copy)
        if step == 0:
            for j in range(bands - 1):
                source = (band + bands - 1 - j) % bands
                remote(small, small_band.at[source], sb_send.at[j], sb_recv.at[j], band=source).wait_recv()
            total = small_band[0]
            for j in range(1, bands):
                total = total + small_band[j]
            small_shard[shard] = total
            for j, peer in enumerate(shard_peers):
                copy = remote(
                    small_shard.at[shard], small_shard.at[shard], ss_send.at[j], ss_recv.at[j], shard=peer
                )
                copy.start()
                waits.append(copy)

    for way in range(2):
        for j in range(1, bands // 2):
            remote(
                done.at[way], others.at[j - 1, way], far_send.at[j - 1, way], far_recv.at[j - 1, way], band=partner
            ).wait_recv()
        total = done[way].astype(F32)
        for j in range(1, bands // 2):
            total = total + others[j - 1, way].astype(F32)
        mixed[core, way] = total.astype(BF)
        copy = remote(
            mixed.at[core, way], mixed.at[core, way], mix_send.at[way], mix_recv.at[way], band=partner
        )
        copy.start()
        waits.append(copy)
    for j in range(count - 1):
        source = (shard + count - 1 - j) % count
        remote(small, small_shard.at[source], ss_send.at[j], ss_recv.at[j], shard=source).wait_recv()
    total = small_shard[0]
    for j in range(1, count):
        total = total + small_shard[j]
    out_small[...] = total
    for way in range(2):
        remote(
            mixed.at[core, way], mixed.at[1 - core, way], mix_send.at[way], mix_recv.at[way], band=partner
        ).wait_recv()
    for quarter in range(4):
        out_att[:, quarter * 512 : quarter * 512 + 512] = mixed[quarter // 2, quarter % 2, 0].astype(F32)
        out_exp[:, quarter * 512 : quarter * 512 + 512] = mixed[quarter // 2, quarter % 2, 1].astype(F32)
        out_red[quarter] = mixed[quarter // 2, quarter % 2, 2].astype(F32)
    for copy in waits:
        copy.wait_send()


def reduce_to_owners(att, exp, red, small):
    count = lax.axis_size("shard")
    bands = lax.axis_size("band")
    rows = att.shape[1]
    dma = pltpu.SemaphoreType.DMA
    far = max(bands // 2 - 1, 1)
    return pl.pallas_call(
        lambda *refs: reduce_kernel(count, bands, *refs),
        out_shape=(
            jax.ShapeDtypeStruct(att.shape[1:], F32),
            jax.ShapeDtypeStruct(exp.shape[1:], F32),
            jax.ShapeDtypeStruct(red.shape[1:], F32),
            jax.ShapeDtypeStruct(small.shape, F32),
        ),
        in_specs=[VM] * 4,
        out_specs=[VM] * 4,
        scratch_shapes=[
            pltpu.VMEM((2, count, 3, rows, 512), BF),
            pltpu.VMEM((2, count - 1, 3, rows, 512), BF),
            pltpu.VMEM((2, count - 1, 3, rows, 512), BF),
            pltpu.VMEM((2, 3, rows, 512), BF),
            pltpu.VMEM((far, 2, 3, rows, 512), BF),
            pltpu.VMEM((2, 2, 3, rows, 512), BF),
            pltpu.VMEM((bands,) + small.shape, F32),
            pltpu.VMEM((count,) + small.shape, F32),
            dma((2, count, 3)), dma((2, count, 3)), dma((2, count - 1)), dma((2, count - 1)),
            dma((far, 2)), dma((far, 2)), dma((2,)), dma((2,)),
            dma((bands - 1,)), dma((bands - 1,)), dma((count - 1,)), dma((count - 1,)),
        ],
        compiler_params=pltpu.CompilerParams(
            collective_id=1, has_side_effects=True, vmem_limit_bytes=48 * 1024 * 1024
        ),
        name="reduce_to_owners",
    )(att, exp, red, small)


def passed_along(block, axis, distance):
    devices = range(lax.axis_size(axis))
    route = [((i - distance) % len(devices), i) for i in devices]
    return lax.ppermute(block, axis, route)


def to_windows(frame):
    image_count, rows_total, cols_total = (frame.shape[0], frame.shape[1], frame.shape[2])
    trailing = frame.shape[3:]
    blocks = frame.reshape((image_count, rows_total // WIN, WIN, cols_total // WIN, WIN) + trailing)
    blocks = jnp.moveaxis(blocks, 3, 2)
    return blocks.reshape(
        (image_count * (rows_total // WIN) * (cols_total // WIN), WIN * WIN) + trailing
    )


def from_windows(blocks, image_count, rows_total, cols_total):
    trailing = blocks.shape[2:]
    frame = blocks.reshape((image_count, rows_total // WIN, cols_total // WIN, WIN, WIN) + trailing)
    frame = jnp.moveaxis(frame, 3, 2)
    return frame.reshape((image_count, rows_total, cols_total) + trailing)


def layer_normalize(values):
    center = jnp.mean(values, axis=-1, keepdims=True)
    centered = values - center
    variance = jnp.mean(centered * centered, axis=-1, keepdims=True)
    inverse_deviation = lax.rsqrt(variance + NORM_EPS)
    return (centered * inverse_deviation, inverse_deviation)


def normalize_backward(gradient_standardized, standardized_input, inverse_deviation):
    return inverse_deviation * (
        gradient_standardized
        - jnp.mean(gradient_standardized, axis=-1, keepdims=True)
        - standardized_input
        * jnp.mean(gradient_standardized * standardized_input, axis=-1, keepdims=True)
    )


def gelu_parts(hidden_pre):
    normal_cdf = 0.5 * (1.0 + lax.erf(hidden_pre * (1.0 / math.sqrt(2.0))))
    density = jnp.exp(-0.5 * hidden_pre * hidden_pre) * (1.0 / math.sqrt(2.0 * math.pi))
    return (hidden_pre * normal_cdf, normal_cdf + hidden_pre * density)


def adamw(weight, grad, first, second, decay):
    first_new = BETA_ONE * first + (1.0 - BETA_ONE) * grad
    second_new = BETA_TWO * second + (1.0 - BETA_TWO) * grad * grad
    corr_one = 1.0 - BETA_ONE**STEP
    corr_two = 1.0 - BETA_TWO**STEP
    step_dir = first_new / corr_one / (jnp.sqrt(second_new / corr_two) + ADAM_EPS)
    return (weight - LEARN_RATE * (step_dir + decay * weight), first_new, second_new)


PADDED = 64
GROUP = 128


def dot_nn(a, b):
    return jnp.dot(a, b, preferred_element_type=F32)


def dot_tn(a, b):
    return lax.dot_general(a, b, (((0,), (0,)), ((), ())), preferred_element_type=F32)


def dot_nt(a, b):
    return lax.dot_general(a, b, (((1,), (1,)), ((), ())), preferred_element_type=F32)


def block_kernel(
    inv_root, x_ref, d_ref, att, exp, red, vec, bias, same,
    out_y, out_dt, g_att, g_exp, g_red, g_vec, g_bias,
    xhat1, q_s, k_s, v_s, h1_s, o_s, do_s, p_s, dqkv_s, r1_s, dr1_s,
):
    rows, width = x_ref.shape
    windows = rows // PADDED
    heads = bias.shape[0]
    head_width = width // heads
    stacked = GROUP // head_width
    groups = width // GROUP
    scale = 1.0 / math.sqrt(head_width)

    def row(k):
        return vec[k : k + 1, :]

    def normed(values):
        centered = values - jnp.mean(values, axis=-1, keepdims=True)
        inverse = lax.rsqrt(jnp.mean(centered * centered, axis=-1, keepdims=True) + NORM_EPS)
        return centered * inverse, inverse

    def put(ref, value, lanes=None):
        value = (value * inv_root).astype(BF)
        if lanes is None:
            ref[...] = value
        else:
            ref[:, lanes] = value

    def column_sum(k, value):
        g_vec[k : k + 1, :] = jnp.sum(value, axis=0, keepdims=True)

    lane = lax.broadcasted_iota(jnp.int32, (1, GROUP), 1) // head_width

    def stack_heads(block):
        zero = jnp.zeros_like(block)
        return jnp.concatenate([jnp.where(lane == h, block, zero) for h in range(stacked)], axis=0)

    def pick_heads(block):
        total = jnp.where(lane == 0, block[:PADDED], 0.0)
        for h in range(1, stacked):
            total = jnp.where(lane == h, block[h * PADDED : (h + 1) * PADDED], total)
        return total

    g_vec[...] = jnp.zeros_like(g_vec)
    standard, inverse1 = normed(x_ref[...].astype(F32))
    xhat1[...] = standard
    h1_s[...] = (standard * (1.0 + row(0)) + row(1)).astype(BF)
    q_s[...] = ((dot_nn(h1_s[...], att[:, :width]) + row(2)) * scale).astype(BF)
    k_s[...] = dot_nn(h1_s[...], att[:, width : 2 * width]).astype(BF)
    v_s[...] = (dot_nn(h1_s[...], att[:, 2 * width : 3 * width]) + row(3)).astype(BF)

    def attend(w, carry):
        here = pl.ds(pl.multiple_of(w * PADDED, PADDED), PADDED)
        allowed = same[w] > 0.5
        allowed = jnp.concatenate([same[w]] * stacked, axis=0) > 0.5
        for g in range(groups):
            lanes = slice(g * GROUP, (g + 1) * GROUP)
            scores = dot_nt(stack_heads(q_s[here, lanes]), k_s[here, lanes])
            shift = jnp.concatenate([bias[g * stacked + h] for h in range(stacked)], axis=0)
            scores = jnp.where(allowed, scores + shift, MASK_VALUE)
            powers = jnp.exp(scores - jnp.max(scores, axis=-1, keepdims=True))
            prob = powers / jnp.sum(powers, axis=-1, keepdims=True)
            p_s[w, g] = prob
            o_s[here, lanes] = pick_heads(dot_nn(prob.astype(BF), v_s[here, lanes])).astype(BF)
        return carry

    lax.fori_loop(0, windows, attend, 0)

    r1_s[...] = x_ref[...].astype(F32) + dot_nn(o_s[...], att[:, 3 * width :]) + row(4)
    xhat2, inverse2 = normed(r1_s[...])
    h2 = (xhat2 * (1.0 + row(5)) + row(6)).astype(BF)
    d_b = d_ref[...]
    d = d_b.astype(F32)
    column_sum(7, d)
    out_y[...] = r1_s[...] + row(7)
    chunks = exp.shape[1] // width
    for c in range(chunks):
        lanes = slice(c * width, (c + 1) * width)
        pre = dot_nn(h2, exp[:, lanes]) + row(8 + c)
        activated, slope = gelu_parts(pre)
        z = activated.astype(BF)
        out_y[...] += dot_nn(z, red[lanes, :])
        g_red[lanes, :] = (dot_tn(z, d_b) * inv_root).astype(BF)
        de = dot_nt(d_b, red[lanes, :]) * slope
        column_sum(8 + c, de)
        deb = de.astype(BF)
        put(g_exp, dot_tn(h2, deb), lanes)
        term = dot_nt(deb, exp[:, lanes])
        if c == 0:
            dr1_s[...] = term
        else:
            dr1_s[...] += term
    dh2 = dr1_s[...]
    column_sum(5, dh2 * xhat2)
    column_sum(6, dh2)
    dr1 = d + normalize_backward(dh2 * (1.0 + row(5)), xhat2, inverse2)
    dr1_s[...] = dr1
    column_sum(4, dr1)
    dr1b = dr1.astype(BF)
    put(g_att, dot_tn(o_s[...], dr1b), slice(3 * width, 4 * width))
    do_s[...] = dot_nt(dr1b, att[:, 3 * width :]).astype(BF)
    g_bias[...] = jnp.zeros_like(g_bias)

    def attend_back(w, carry):
        here = pl.ds(pl.multiple_of(w * PADDED, PADDED), PADDED)
        for g in range(groups):
            lanes = slice(g * GROUP, (g + 1) * GROUP)
            prob = p_s[w, g]
            grads = stack_heads(do_s[here, lanes])
            dp = dot_nt(grads, v_s[here, lanes])
            dv = dot_tn(prob.astype(BF), grads)
            ds = prob * (dp - jnp.sum(prob * dp, axis=-1, keepdims=True))
            for h in range(stacked):
                g_bias[g * stacked + h] += ds[h * PADDED : (h + 1) * PADDED]
            dsb = ds.astype(BF)
            dq = pick_heads(dot_nn(dsb, k_s[here, lanes])) * scale
            dk = dot_tn(dsb, stack_heads(q_s[here, lanes]))
            g_vec[2:3, lanes] += jnp.sum(dq, axis=0, keepdims=True)
            g_vec[3:4, lanes] += jnp.sum(dv, axis=0, keepdims=True)
            dqkv_s[here, lanes] = dq.astype(BF)
            dqkv_s[here, width + g * GROUP : width + (g + 1) * GROUP] = dk.astype(BF)
            dqkv_s[here, 2 * width + g * GROUP : 2 * width + (g + 1) * GROUP] = dv.astype(BF)
        return carry

    lax.fori_loop(0, windows, attend_back, 0)

    for c in range(3):
        lanes = slice(c * width, (c + 1) * width)
        put(g_att, dot_tn(h1_s[...], dqkv_s[:, lanes]), lanes)
    dh1 = dot_nt(dqkv_s[...], att[:, : 3 * width])
    column_sum(0, dh1 * xhat1[...])
    column_sum(1, dh1)
    out_dt[...] = dr1_s[...] + normalize_backward(dh1 * (1.0 + row(0)), xhat1[...], inverse1)


def block_on_windows(windows_in, grad_windows, matrices, row_vectors, pos_bias, same, inv_root):
    count, size, width = windows_in.shape
    rows = count * PADDED
    heads = pos_bias.shape[0]

    def padded(blocks):
        return jnp.pad(blocks, ((0, 0), (0, PADDED - size), (0, 0))).reshape(rows, width)

    attention, expand, shrink = matrices
    vm = pltpu.VMEM
    return pl.pallas_call(
        lambda *refs: block_kernel(inv_root, *refs),
        out_shape=(
            jax.ShapeDtypeStruct((rows, width), F32),
            jax.ShapeDtypeStruct((rows, width), F32),
            jax.ShapeDtypeStruct(attention.shape, BF),
            jax.ShapeDtypeStruct(expand.shape, BF),
            jax.ShapeDtypeStruct(shrink.shape, BF),
            jax.ShapeDtypeStruct((16, width), F32),
            jax.ShapeDtypeStruct(pos_bias.shape, F32),
        ),
        in_specs=[VM] * 8,
        out_specs=[VM] * 7,
        scratch_shapes=[
            vm((rows, width), F32), vm((rows, width), BF), vm((rows, width), BF), vm((rows, width), BF),
            vm((rows, width), BF), vm((rows, width), BF), vm((rows, width), BF),
            vm((count, width // GROUP, GROUP * heads // width * PADDED, PADDED), F32),
            vm((rows, 3 * width), BF), vm((rows, width), F32), vm((rows, width), F32),
        ],
        compiler_params=pltpu.CompilerParams(vmem_limit_bytes=48 * 1024 * 1024),
        name="block_on_windows",
    )(padded(windows_in), padded(grad_windows), attention, expand, shrink, row_vectors, pos_bias, same)


def on_device(
    block_input,
    output_grad,
    region_ids,
    relative_index,
    attention_weight,
    expand_weight,
    reduce_weight,
    vectors,
    bias_table,
    attention_mean,
    attention_square,
    expand_mean,
    expand_square,
    reduce_mean,
    reduce_square,
    vectors_mean,
    vectors_square,
    table_mean,
    table_square,
):
    image_count, band_rows, columns, features = block_input.shape
    window_size = WIN * WIN
    shard_count = lax.axis_size("shard")
    band_count = lax.axis_size("band")
    edge_rows = jnp.stack([block_input[:, :SHIFT], output_grad[:, :SHIFT]])
    rows_below = passed_along(edge_rows, "band", -1)
    inner_rows = jnp.stack([block_input[:, SHIFT:], output_grad[:, SHIFT:]])
    shifted = jnp.roll(jnp.concatenate([inner_rows, rows_below], axis=2), -SHIFT, axis=3)
    windows_in = to_windows(shifted[0])
    grad_windows = to_windows(shifted[1])
    pad = PADDED - window_size
    region_windows = jnp.tile(to_windows(region_ids[None]), (image_count, 1))
    region_windows = jnp.pad(region_windows, ((0, 0), (0, pad)), constant_values=-1)
    same_region = (region_windows[:, :, None] == region_windows[:, None, :]).astype(F32)
    table_rows = bias_table.shape[0]
    head_count = bias_table.shape[1]
    padded_index = jnp.pad(relative_index, ((0, pad), (0, pad)), constant_values=-1)
    one_hot = (
        padded_index.reshape(-1)[:, None] == jnp.arange(table_rows, dtype=jnp.int32)[None, :]
    ).astype(jnp.float32)
    pos_bias = jnp.dot(one_hot, bias_table, precision=lax.Precision.HIGHEST).T.reshape(
        head_count, PADDED, PADDED
    )
    feature_rows = attention_weight.shape[0]
    gathered = gather_shards(
        attention_weight.astype(BF),
        expand_weight.astype(BF),
        reduce_weight.astype(BF).reshape(4, feature_rows, features),
        jnp.pad(vectors.astype(BF), ((0, 4), (0, 128 - vectors.shape[1]))),
    )
    matrices = (
        gathered[0].reshape(features, -1),
        gathered[1].reshape(features, -1),
        gathered[2].reshape(-1, features),
    )
    row_vectors_list = (
        jnp.moveaxis(gathered[3][:, :12, : vectors.shape[1]], 0, 1).reshape(12, features).astype(jnp.float32)
    )
    inv_root = 1.0 / math.sqrt(image_count * shard_count * band_rows * band_count * columns)
    output_rows, gradient_token_rows, grad_attention, grad_expand, grad_shrink, grad_vectors, grad_posbias = (
        block_on_windows(
            windows_in, grad_windows, matrices, jnp.pad(row_vectors_list, ((0, 4), (0, 0))), pos_bias,
            same_region, inv_root,
        )
    )
    output_rows = output_rows.reshape(-1, PADDED, features)[:, :window_size]
    gradient_token_rows = gradient_token_rows.reshape(-1, PADDED, features)[:, :window_size]
    grad_vectors = grad_vectors[:12]
    table_local = jnp.dot(
        grad_posbias.reshape(head_count, -1), one_hot, precision=lax.Precision.HIGHEST
    ).T
    vector_terms = grad_vectors.size
    small = jnp.concatenate([grad_vectors.reshape(-1), table_local.reshape(-1)]) * inv_root
    small_rows = -(-small.size // 1024) * 8
    small = jnp.pad(small, (0, small_rows * 128 - small.size)).reshape(small_rows, 128)
    attention_grad, expand_grad, reduce_grad, small_sum = reduce_to_owners(
        grad_attention.reshape(shard_count, feature_rows, -1),
        grad_expand.reshape(shard_count, feature_rows, -1),
        grad_shrink.reshape(shard_count, 4, feature_rows, features),
        small,
    )
    reduce_grad = reduce_grad.reshape(reduce_weight.shape)
    small_sum = small_sum.reshape(-1)
    vectors_grad = lax.dynamic_slice_in_dim(
        small_sum[:vector_terms].reshape(12, features),
        lax.axis_index("shard") * vectors.shape[1],
        vectors.shape[1],
        axis=1,
    )
    table_grad = small_sum[vector_terms : vector_terms + bias_table.size].reshape(bias_table.shape)
    frames = jnp.stack(
        [
            from_windows(
                output_rows.reshape(-1, window_size, features), image_count, band_rows, columns
            ),
            from_windows(
                gradient_token_rows.reshape(-1, window_size, features),
                image_count,
                band_rows,
                columns,
            ),
        ]
    )
    frames = jnp.roll(frames, SHIFT, axis=3)
    rows_above = passed_along(
        frames[:, :, band_rows - SHIFT :].astype(jnp.bfloat16), "band", 1
    ).astype(jnp.float32)
    placed = jnp.concatenate([rows_above, frames[:, :, : band_rows - SHIFT]], axis=2)
    new_attention, new_attention_mean, new_attention_square = adamw(
        attention_weight, attention_grad, attention_mean, attention_square, WEIGHT_DECAY
    )
    new_expand, new_expand_mean, new_expand_square = adamw(
        expand_weight, expand_grad, expand_mean, expand_square, WEIGHT_DECAY
    )
    new_reduce, new_reduce_mean, new_reduce_square = adamw(
        reduce_weight, reduce_grad, reduce_mean, reduce_square, WEIGHT_DECAY
    )
    new_vectors, new_vectors_mean, new_vectors_square = adamw(
        vectors, vectors_grad, vectors_mean, vectors_square, 0.0
    )
    new_table, new_table_mean, new_table_square = adamw(
        bias_table, table_grad, table_mean, table_square, 0.0
    )
    return (
        placed[0],
        placed[1],
        attention_grad,
        expand_grad,
        reduce_grad,
        vectors_grad,
        table_grad,
        new_attention,
        new_expand,
        new_reduce,
        new_vectors,
        new_table,
        new_attention_mean,
        new_attention_square,
        new_expand_mean,
        new_expand_square,
        new_reduce_mean,
        new_reduce_square,
        new_vectors_mean,
        new_vectors_square,
        new_table_mean,
        new_table_square,
    )


def solution(mesh):
    return jax.shard_map(
        on_device,
        mesh=mesh,
        in_specs=(
            P("shard", "band", None, None),
            P("shard", "band", None, None),
            P("band", None),
            P(),
            P("shard", None),
            P("shard", None),
            P("shard", None),
            P(None, "shard"),
            P(),
            P("shard", None),
            P("shard", None),
            P("shard", None),
            P("shard", None),
            P("shard", None),
            P("shard", None),
            P(None, "shard"),
            P(None, "shard"),
            P(),
            P(),
        ),
        out_specs=(
            P("shard", "band", None, None),
            P("shard", "band", None, None),
            P("shard", None),
            P("shard", None),
            P("shard", None),
            P(None, "shard"),
            P(),
            P("shard", None),
            P("shard", None),
            P("shard", None),
            P(None, "shard"),
            P(),
            P("shard", None),
            P("shard", None),
            P("shard", None),
            P("shard", None),
            P("shard", None),
            P("shard", None),
            P(None, "shard"),
            P(None, "shard"),
            P(),
            P(),
        ),
        check_vma=False,
    )
```

profile of v0, /device:TPU:25, one launch (start us, length us, event | category | flops | bytes accessed | tf_op | source)
XLA Modules:
  0.0 163.9 jit_solution(12198295444306248291)
XLA Ops:
  0.7 0.9 slice_bitcast_fusion.2
  2.4 1.0 slice_bitcast_fusion
  3.4 1.1 convert_element_type.38
  4.6 47.6 %gather_shards.1 = (bf16[8,64,2048]{2,1,0:T(8,128)(2,1)S(1)}, bf16[8,64,2048]{2,1,0:T(8,128)(2,1)S(1)}, bf16[8,4,64,512]{3,2,1,0:T(8,128)(2,1)}, bf16[8,16,128]{2,1,0:T(8,128)(2,1)S(1)}) custom-call(bf16[64,2048]{1,0:T(8,128)(2,1)S(1)} %convert_element_type.36.refs_0_, bf16[64,2048]{1,0:T(8,128)(2,1)S(1)} %convert_element_type.37.refs_1_, ...), custom_call_target="tpu_custom_call" | custom-call | tf_op jit(solution)/shard_map/gather_shards/pallas_call | solution.py:147
  52.3 1.4 copy-done
  53.7 1.4 copy-done.1
  55.3 1.0 convolution_bitcast_fusion
  57.6 19.9 %block_on_windows.1 = (f32[256,512]{1,0:T(8,128)S(1)}, f32[256,512]{1,0:T(8,128)S(1)}, bf16[512,2048]{1,0:T(8,128)(2,1)S(1)}, bf16[512,2048]{1,0:T(8,128)(2,1)},...) custom-call(bf16[256,512]{1,0:T(8,128)(2,1)S(1)} %bitcast.53, ...), custom_call_target="tpu_custom_call" | custom-call | tf_op jit(solution)/shard_map/block_on_windows/pallas_call | solution.py:555
  77.5 1.4 copy-done.2
  79.1 1.4 fusion
  80.6 1.6 copy-done.3
  82.2 1.6 copy-done.4
  83.8 59.7 %reduce_to_owners.1 = (f32[64,2048]{1,0:T(8,128)S(1)}, f32[64,2048]{1,0:T(8,128)S(1)}, f32[4,64,512]{2,1,0:T(8,128)S(1)}, f32[72,128]{1,0:T(8,128)S(1)}) custom-call(bf16[8,64,2048]{2,1,0:T(8,128)(2,1)S(1)} %bitcast.50, bf16[8,64,2048]{2,1,0:T(8,128)(2,1)S(1)} %bitcast.51, bf16[8,4,64,512]{3,2,1,0:T(8,128)(2,1)} %bitcast.59, ...), custom_call_target="tpu_custom_call" | custom-call | tf_op jit(solution)/shard_map/reduce_to_owners/pallas_call | solution.py:309
  144.3 0.9 copy.118
  145.3 0.8 slice.93
  146.1 1.1 reshape.146
  147.5 1.2 copy.110
  149.5 1.8 %fusion.3 = f32[2,1,14,14,512]{4,0,3,2,1:T(2,128)S(1)} fusion(f32[1,1,14,14,512]{4,0,3,2,1:T(1,128)S(1)} %bitcast.61, f32[1,1,14,14,512]{4,0,3,2,1:T(1,128)} %bitcast.60), kind=kLoop, calls=%fused_computation.6 | loop fusion | flops 602112 | bytes 1605632 | tf_op jit(solution)/shard_map/jit(_roll_static)/concatenate | solution.py:683
  151.4 2.2 %collective-permute-start.1 = (bf16[2,1,3,14,512]{4,0,3,2,1:T(2,128)(2,1)S(1)}, bf16[2,1,3,14,512]{4,0,3,2,1:T(2,128)(2,1)S(1)}, u32[]{:S(2)}, u32[]{:S(2)}) collective-permute-start(bf16[2,1,3,14,512]{4,0,3,2,1:T(2,128)(2,1)S(1)} %slice.116), channel_id=1, source_target_pairs={{24,0},{0,8},{8,16},{16,24},{25,1},{1,9},{9,17},{17,25},{26,2},{2,... | collective-permute-start | bytes 258056 | tf_op jit(solution)/shard_map/ppermute | solution.py:342
  153.6 1.4 multiply_subtract_fusion.2
  155.1 1.4 multiply_subtract_fusion.1
  157.0 1.4 multiply_subtract_fusion
  160.0 1.5 fusion.9
  161.6 0.8 copy.136
  (96 shorter events, 8.2 us)
Async XLA Ops:
  0.7 3.8 %copy-start.5 = (f32[64,2048]{1,0:T(8,128)S(1)}, f32[64,2048]{1,0:T(8,128)}, u32[]{:S(2)}) copy-start(f32[64,2048]{1,0:T(8,128)} %param.23) | copy-start | bytes 1572868
  0.7 3.9 %copy-start.6 = (f32[64,2048]{1,0:T(8,128)S(1)}, f32[64,2048]{1,0:T(8,128)}, u32[]{:S(2)}) copy-start(f32[64,2048]{1,0:T(8,128)} %param.24) | copy-start | bytes 1572868
  0.7 3.9 %copy-start.16 = (f32[12,64]{1,0:T(8,128)S(1)}, f32[12,64]{1,0:T(8,128)}, u32[]{:S(2)}) copy-start(f32[12,64]{1,0:T(8,128)} %param.26) | copy-start | bytes 9220
  1.6 53.6 %copy-start.17 = (s32[49,49]{1,0:T(8,128)S(1)}, s32[49,49]{1,0:T(8,128)}, u32[]{:S(2)}) copy-start(s32[49,49]{1,0:T(8,128)} %param.22) | copy-start | bytes 28816
  1.6 53.6 %copy-start.18 = (f32[169,16]{0,1:T(8,128)S(1)}, f32[169,16]{0,1:T(8,128)}, u32[]{:S(2)}) copy-start(f32[169,16]{0,1:T(8,128)} %param.27) | copy-start | bytes 32452
  1.6 55.2 %collective-permute-start = (bf16[2,1,3,14,512]{4,3,2,1,0:T(8,128)(2,1)S(1)}, bf16[2,1,3,14,512]{4,3,2,1,0:T(8,128)(2,1)S(1)}, u32[]{:S(2)}, u32[]{:S(2)}) collective-permute-start(bf16[2,1,3,14,512]{4,3,2,1,0:T(8,128)(2,1)S(1)} %pad_maximum_fusion.6), channel_id=1, source_target_pairs={{8,0},{16,8},{24,16},{0,24},{9,1},{17,9},{25,17},{1,25},{10,2},{18... | collective-permute-start | bytes 258056 | tf_op jit(solution)/shard_map/ppermute | solution.py:342
  4.5 52.0 %copy-start.21 = (s32[14,14]{1,0:T(8,128)S(1)}, s32[14,14]{1,0:T(8,128)}, u32[]{:S(2)}) copy-start(s32[14,14]{1,0:T(8,128)} %param.21) | copy-start | bytes 2356
  52.3 1.4 copy-start
  80.6 1.6 copy-start.3
  82.2 1.6 copy-start.4
  145.2 13.2 %copy-start.15 = (f32[169,16]{0,1:T(8,128)}, f32[169,16]{0,1:T(8,128)S(1)}, u32[]{:S(2)}) copy-start(f32[169,16]{0,1:T(8,128)S(1)} %copy.118) | copy-start | bytes 32452
  148.8 4.9 %copy-start.9 = (f32[64,2048]{1,0:T(8,128)S(1)}, f32[64,2048]{1,0:T(8,128)}, u32[]{:S(2)}) copy-start(f32[64,2048]{1,0:T(8,128)} %param.28) | copy-start | bytes 1572868
  148.8 4.9 %copy-start.10 = (f32[64,2048]{1,0:T(8,128)S(1)}, f32[64,2048]{1,0:T(8,128)}, u32[]{:S(2)}) copy-start(f32[64,2048]{1,0:T(8,128)} %param.29) | copy-start | bytes 1572868
  151.3 3.8 %copy-start.7 = (f32[64,2048]{1,0:T(8,128)S(1)}, f32[64,2048]{1,0:T(8,128)}, u32[]{:S(2)}) copy-start(f32[64,2048]{1,0:T(8,128)} %param.24) | copy-start | bytes 1572868
  151.3 3.8 %copy-start.11 = (f32[64,2048]{1,0:T(8,128)S(1)}, f32[64,2048]{1,0:T(8,128)}, u32[]{:S(2)}) copy-start(f32[64,2048]{1,0:T(8,128)} %param.30) | copy-start | bytes 1572868
  151.3 3.8 %copy-start.12 = (f32[64,2048]{1,0:T(8,128)S(1)}, f32[64,2048]{1,0:T(8,128)}, u32[]{:S(2)}) copy-start(f32[64,2048]{1,0:T(8,128)} %param.31) | copy-start | bytes 1572868
  151.4 8.6 %collective-permute-start.1 = (bf16[2,1,3,14,512]{4,0,3,2,1:T(2,128)(2,1)S(1)}, bf16[2,1,3,14,512]{4,0,3,2,1:T(2,128)(2,1)S(1)}, u32[]{:S(2)}, u32[]{:S(2)}) collective-permute-start(bf16[2,1,3,14,512]{4,0,3,2,1:T(2,128)(2,1)S(1)} %slice.116), channel_id=1, source_target_pairs={{24,0},{0,8},{8,16},{16,24},{25,1},{1,9},{9,17},{17,25},{26,2},{2,... | collective-permute-start | bytes 258056 | tf_op jit(solution)/shard_map/ppermute | solution.py:342
  155.1 1.5 copy-start.8
  155.1 1.5 copy-start.13
  155.1 1.9 %copy-start.14 = (f32[256,512]{1,0:T(8,128)S(1)}, f32[256,512]{1,0:T(8,128)}, u32[]{:S(2)}) copy-start(f32[256,512]{1,0:T(8,128)} %param.33) | copy-start | bytes 1572868
  156.5 1.9 %copy-start.19 = (f32[169,16]{0,1:T(8,128)S(1)}, f32[169,16]{0,1:T(8,128)}, u32[]{:S(2)}) copy-start(f32[169,16]{0,1:T(8,128)} %param.36) | copy-start | bytes 32452
  156.5 1.9 %copy-start.20 = (f32[169,16]{0,1:T(8,128)S(1)}, f32[169,16]{0,1:T(8,128)}, u32[]{:S(2)}) copy-start(f32[169,16]{0,1:T(8,128)} %param.37) | copy-start | bytes 32452
  156.5 2.6 %copy-start.22 = (f32[12,64]{1,0:T(8,128)S(1)}, f32[12,64]{1,0:T(8,128)}, u32[]{:S(2)}) copy-start(f32[12,64]{1,0:T(8,128)} %param.34) | copy-start | bytes 9220
  156.5 2.6 %copy-start.23 = (f32[12,64]{1,0:T(8,128)S(1)}, f32[12,64]{1,0:T(8,128)}, u32[]{:S(2)}) copy-start(f32[12,64]{1,0:T(8,128)} %param.35) | copy-start | bytes 9220
  (2 other events, 2.8 us)
where the time goes:
time: 164 us
  Pallas kernels  127 us (77%)
  local copies, waits for them, and re-layouts  19.8 us (12%)
  other arithmetic  10.4 us (6%)
  starting transfers between devices  2.96 us (2%)
  matrix products  2.43 us (1%)
    pallas_call x1, Pallas kernels, reduce_to_owners(): pl.pallas_call(lambda *refs: reduce_kernel(count, bands, *refs), out_shap...  59.7 us
    pallas_call x1, Pallas kernels, gather_shards(): pl.pallas_call(lambda *refs: gather_kernel(count, *refs), out_shape=(jax....  47.6 us
    pallas_call x1, Pallas kernels, block_on_windows(): pl.pallas_call(lambda *refs: block_kernel(inv_root, *refs), out_shape=(ja...  19.9 us
    unnamed x56, local copies, waits for them, and re-layouts  11.4 us
    sub x5, other arithmetic, adamw(): weight - LEARN_RATE * (step_dir + decay * weight)  5.58 us
  transfers between devices with their start and end apart: 2, of which 0 were waited for; matrix products, arithmetic and copies ran while one was open for 6% of the time, Pallas kernels for 29%

commit v1 on v0

--- a/solution.py
+++ b/solution.py
@@ -159,7 +159,7 @@
             dma((count - 1,)), dma((count - 1,)), dma((4,)),
         ],
         compiler_params=pltpu.CompilerParams(
-            collective_id=0, has_side_effects=True, vmem_limit_bytes=48 * 1024 * 1024
+            collective_id=0, has_side_effects=True, vmem_limit_bytes=12 * 1024 * 1024
         ),
         name="gather_shards",
     )(att, exp, red, vec)
@@ -330,7 +330,7 @@
             dma((bands - 1,)), dma((bands - 1,)), dma((count - 1,)), dma((count - 1,)),
         ],
         compiler_params=pltpu.CompilerParams(
-            collective_id=1, has_side_effects=True, vmem_limit_bytes=48 * 1024 * 1024
+            collective_id=1, has_side_effects=True, vmem_limit_bytes=24 * 1024 * 1024
         ),
         name="reduce_to_owners",
     )(att, exp, red, small)
@@ -460,7 +460,6 @@
 
     def attend(w, carry):
         here = pl.ds(pl.multiple_of(w * PADDED, PADDED), PADDED)
-        allowed = same[w] > 0.5
         allowed = jnp.concatenate([same[w]] * stacked, axis=0) > 0.5
         for g in range(groups):
             lanes = slice(g * GROUP, (g + 1) * GROUP)
@@ -571,7 +570,7 @@
             vm((count, width // GROUP, GROUP * heads // width * PADDED, PADDED), F32),
             vm((rows, 3 * width), BF), vm((rows, width), F32), vm((rows, width), F32),
         ],
-        compiler_params=pltpu.CompilerParams(vmem_limit_bytes=48 * 1024 * 1024),
+        compiler_params=pltpu.CompilerParams(vmem_limit_bytes=28 * 1024 * 1024),
         name="block_on_windows",
     )(padded(windows_in), padded(grad_windows), attention, expand, shrink, row_vectors, pos_bias, same)
 

time: 164 us -> 166 us (1.012)
  local copies, waits for them, and re-layouts: 19.8 us -> 27.7 us
  Pallas kernels: 127 us -> 121 us
    unnamed x56 -> x90, local copies, waits for them, and re-layouts: 11.4 us -> 22.4 us
    pallas_call x1, Pallas kernels: 19.9 us -> 16.3 us  [block_on_windows(): pl.pallas_call(lambda *refs: block_kernel(inv_root, *refs), out_shape=(ja...]
  transfers between devices with their start and end apart: 2 -> 2, of which waited for: 0 -> 0; matrix products, arithmetic and copies ran while one was open for 6% -> 6% of each run, Pallas kernels for 29% -> 28%
where the time goes in v1:
time: 166 us
  Pallas kernels  121 us (73%)
  local copies, waits for them, and re-layouts  27.7 us (17%)
  other arithmetic  10.6 us (6%)
  starting transfers between devices  2.88 us (2%)
  matrix products  2.43 us (1%)
    pallas_call x1, Pallas kernels, reduce_to_owners(): pl.pallas_call(lambda *refs: reduce_kernel(count, bands, *refs), out_shap...  58.1 us
    pallas_call x1, Pallas kernels, gather_shards(): pl.pallas_call(lambda *refs: gather_kernel(count, *refs), out_shape=(jax....  46.3 us
    unnamed x90, local copies, waits for them, and re-layouts  22.4 us
    pallas_call x1, Pallas kernels, block_on_windows(): pl.pallas_call(lambda *refs: block_kernel(inv_root, *refs), out_shape=(ja...  16.3 us
    sub x5, other arithmetic, adamw(): weight - LEARN_RATE * (step_dir + decay * weight)  5.6 us
  transfers between devices with their start and end apart: 2, of which 0 were waited for; matrix products, arithmetic and copies ran while one was open for 6% of the time, Pallas kernels for 28%

profile of v1, /device:TPU:25, one launch (start us, length us, event | category | flops | bytes accessed | tf_op | source)
XLA Modules:
  0.0 165.5 jit_solution(5294435567243481158)
XLA Ops:
  0.7 0.9 slice_bitcast_fusion.2
  2.9 1.0 slice_bitcast_fusion
  4.0 1.1 convert_element_type.38
  5.2 46.3 %gather_shards.1 = (bf16[8,64,2048]{2,1,0:T(8,128)(2,1)S(1)}, bf16[8,64,2048]{2,1,0:T(8,128)(2,1)S(1)}, bf16[8,4,64,512]{3,2,1,0:T(8,128)(2,1)S(1)}, bf16[8,16,128]{2,1,0:T(8,128)(2,1)S(1)}) custom-call(bf16[64,2048]{1,0:T(8,128)(2,1)S(1)} %convert_element_type.36.refs_0_, bf16[64,2048]{1,0:T(8,128)(2,1)S(1)} %convert_element_type.37.refs_1_, ...), custom_call_target="tpu_custom_call" | custom-call | tf_op jit(solution)/shard_map/gather_shards/pallas_call | solution.py:147
  51.5 1.3 copy-done
  52.8 1.4 copy-done.2
  54.4 1.0 convolution_bitcast_fusion
  57.9 1.0 reshape.145
  59.0 1.6 copy-done.1
  60.6 1.6 copy-done.3
  62.9 16.3 %block_on_windows.1 = (f32[256,512]{1,0:T(8,128)S(1)}, f32[256,512]{1,0:T(8,128)S(1)}, bf16[512,2048]{1,0:T(8,128)(2,1)S(1)}, bf16[512,2048]{1,0:T(8,128)(2,1)S(...) custom-call(bf16[256,512]{1,0:T(8,128)(2,1)S(1)} %bitcast.55, ...), custom_call_target="tpu_custom_call" | custom-call | tf_op jit(solution)/shard_map/block_on_windows/pallas_call | solution.py:554
  79.2 1.3 copy-done.4
  80.6 1.4 copy-done.6
  81.9 1.4 copy-done.8
  85.7 1.4 fusion
  87.2 1.6 copy-done.5
  88.8 1.6 copy-done.7
  90.4 1.6 copy-done.9
  92.0 58.1 %reduce_to_owners.1 = (f32[64,2048]{1,0:T(8,128)S(1)}, f32[64,2048]{1,0:T(8,128)S(1)}, f32[4,64,512]{2,1,0:T(8,128)S(1)}, f32[72,128]{1,0:T(8,128)S(1)}) custom-call(bf16[8,64,2048]{2,1,0:T(8,128)(2,1)S(1)} %bitcast.51, bf16[8,64,2048]{2,1,0:T(8,128)(2,1)S(1)} %bitcast.52, bf16[8,4,64,512]{3,2,1,0:T(8,128)(2,1)S(1)} %bitcast.53, ...), custom_call_target="tpu_custom_call" | custom-call | tf_op jit(solution)/shard_map/reduce_to_owners/pallas_call | solution.py:309
  153.0 2.2 %collective-permute-start.1 = (bf16[2,1,3,14,512]{4,0,3,2,1:T(2,128)(2,1)S(1)}, bf16[2,1,3,14,512]{4,0,3,2,1:T(2,128)(2,1)S(1)}, u32[]{:S(2)}, u32[]{:S(2)}) collective-permute-start(bf16[2,1,3,14,512]{4,0,3,2,1:T(2,128)(2,1)S(1)} %slice.116), channel_id=1, source_target_pairs={{24,0},{0,8},{8,16},{16,24},{25,1},{1,9},{9,17},{17,25},{26,2},{2,... | collective-permute-start | bytes 258056 | tf_op jit(solution)/shard_map/ppermute | solution.py:342
  155.2 1.4 multiply_subtract_fusion.2
  156.7 1.4 multiply_subtract_fusion.1
  158.5 1.4 multiply_subtract_fusion
  161.6 1.5 fusion.9
  (130 shorter events, 14.5 us)
Async XLA Ops:
  0.7 4.4 %copy-start.17 = (f32[64,2048]{1,0:T(8,128)S(1)}, f32[64,2048]{1,0:T(8,128)}, u32[]{:S(2)}) copy-start(f32[64,2048]{1,0:T(8,128)} %param.23) | copy-start | bytes 1572868
  0.7 4.5 %copy-start.19 = (f32[64,2048]{1,0:T(8,128)S(1)}, f32[64,2048]{1,0:T(8,128)}, u32[]{:S(2)}) copy-start(f32[64,2048]{1,0:T(8,128)} %param.24) | copy-start | bytes 1572868
  0.7 4.5 %copy-start.29 = (f32[12,64]{1,0:T(8,128)S(1)}, f32[12,64]{1,0:T(8,128)}, u32[]{:S(2)}) copy-start(f32[12,64]{1,0:T(8,128)} %param.26) | copy-start | bytes 9220
  1.6 52.7 %copy-start.31 = (s32[49,49]{1,0:T(8,128)S(1)}, s32[49,49]{1,0:T(8,128)}, u32[]{:S(2)}) copy-start(s32[49,49]{1,0:T(8,128)} %param.22) | copy-start | bytes 28816
  2.3 52.1 %copy-start.32 = (f32[169,16]{0,1:T(8,128)S(1)}, f32[169,16]{0,1:T(8,128)}, u32[]{:S(2)}) copy-start(f32[169,16]{0,1:T(8,128)} %param.27) | copy-start | bytes 32452
  2.3 54.3 %collective-permute-start = (bf16[2,1,3,14,512]{4,3,2,1,0:T(8,128)(2,1)}, bf16[2,1,3,14,512]{4,3,2,1,0:T(8,128)(2,1)S(1)}, u32[]{:S(2)}, u32[]{:S(2)}) collective-permute-start(bf16[2,1,3,14,512]{4,3,2,1,0:T(8,128)(2,1)} %pad_maximum_fusion.6), channel_id=1, source_target_pairs={{8,0},{16,8},{24,16},{0,24},{9,1},{17,9},{25,17},{1,25},{10,2},{18... | collective-permute-start | bytes 258056 | tf_op jit(solution)/shard_map/ppermute | solution.py:342
  5.1 50.6 %copy-start.38 = (s32[14,14]{1,0:T(8,128)S(1)}, s32[14,14]{1,0:T(8,128)}, u32[]{:S(2)}) copy-start(s32[14,14]{1,0:T(8,128)} %param.21) | copy-start | bytes 2356
  54.4 2.4 %copy-start.36 = (s32[4096]{0:T(1024)}, s32[4096]{0:T(1024)S(1)}, u32[]{:S(2)}) copy-start(s32[4096]{0:T(1024)S(1)} %eq.28) | copy-start | bytes 49156
  62.9 22.8 %copy-start.37 = (s32[4096]{0:T(1024)S(1)}, s32[4096]{0:T(1024)}, u32[]{:S(2)}) copy-start(s32[4096]{0:T(1024)} %copy-done.36) | copy-start | bytes 49156
  92.0 58.4 %copy-start.13 = (f32[256,512]{1,0:T(8,128)S(1)}, f32[256,512]{1,0:T(8,128)}, u32[]{:S(2)}) copy-start(f32[256,512]{1,0:T(8,128)} %copy-done.12) | copy-start | bytes 1572868
  150.3 9.6 %copy-start.28 = (f32[169,16]{0,1:T(8,128)}, f32[169,16]{0,1:T(8,128)S(1)}, u32[]{:S(2)}) copy-start(f32[169,16]{0,1:T(8,128)S(1)} %copy.118) | copy-start | bytes 32452
  151.3 3.9 %copy-start.18 = (f32[64,2048]{1,0:T(8,128)S(1)}, f32[64,2048]{1,0:T(8,128)}, u32[]{:S(2)}) copy-start(f32[64,2048]{1,0:T(8,128)} %param.23) | copy-start | bytes 1572868
  151.4 3.8 %copy-start.22 = (f32[64,2048]{1,0:T(8,128)S(1)}, f32[64,2048]{1,0:T(8,128)}, u32[]{:S(2)}) copy-start(f32[64,2048]{1,0:T(8,128)} %param.28) | copy-start | bytes 1572868
  151.4 3.8 %copy-start.23 = (f32[64,2048]{1,0:T(8,128)S(1)}, f32[64,2048]{1,0:T(8,128)}, u32[]{:S(2)}) copy-start(f32[64,2048]{1,0:T(8,128)} %param.29) | copy-start | bytes 1572868
  152.9 3.7 %copy-start.20 = (f32[64,2048]{1,0:T(8,128)S(1)}, f32[64,2048]{1,0:T(8,128)}, u32[]{:S(2)}) copy-start(f32[64,2048]{1,0:T(8,128)} %param.24) | copy-start | bytes 1572868
  152.9 3.7 %copy-start.24 = (f32[64,2048]{1,0:T(8,128)S(1)}, f32[64,2048]{1,0:T(8,128)}, u32[]{:S(2)}) copy-start(f32[64,2048]{1,0:T(8,128)} %param.30) | copy-start | bytes 1572868
  152.9 3.7 %copy-start.25 = (f32[64,2048]{1,0:T(8,128)S(1)}, f32[64,2048]{1,0:T(8,128)}, u32[]{:S(2)}) copy-start(f32[64,2048]{1,0:T(8,128)} %param.31) | copy-start | bytes 1572868
  153.0 8.6 %collective-permute-start.1 = (bf16[2,1,3,14,512]{4,0,3,2,1:T(2,128)(2,1)S(1)}, bf16[2,1,3,14,512]{4,0,3,2,1:T(2,128)(2,1)S(1)}, u32[]{:S(2)}, u32[]{:S(2)}) collective-permute-start(bf16[2,1,3,14,512]{4,0,3,2,1:T(2,128)(2,1)S(1)} %slice.116), channel_id=1, source_target_pairs={{24,0},{0,8},{8,16},{16,24},{25,1},{1,9},{9,17},{17,25},{26,2},{2,... | collective-permute-start | bytes 258056 | tf_op jit(solution)/shard_map/ppermute | solution.py:342
  156.6 1.9 %copy-start.27 = (f32[256,512]{1,0:T(8,128)S(1)}, f32[256,512]{1,0:T(8,128)}, u32[]{:S(2)}) copy-start(f32[256,512]{1,0:T(8,128)} %param.33) | copy-start | bytes 1572868
  158.1 1.9 %copy-start.34 = (f32[169,16]{0,1:T(8,128)S(1)}, f32[169,16]{0,1:T(8,128)}, u32[]{:S(2)}) copy-start(f32[169,16]{0,1:T(8,128)} %param.36) | copy-start | bytes 32452
  158.1 1.9 %copy-start.35 = (f32[169,16]{0,1:T(8,128)S(1)}, f32[169,16]{0,1:T(8,128)}, u32[]{:S(2)}) copy-start(f32[169,16]{0,1:T(8,128)} %param.37) | copy-start | bytes 32452
  158.1 2.6 %copy-start.30 = (f32[12,64]{1,0:T(8,128)S(1)}, f32[12,64]{1,0:T(8,128)}, u32[]{:S(2)}) copy-start(f32[12,64]{1,0:T(8,128)} %param.26) | copy-start | bytes 9220
  158.1 2.5 %copy-start.39 = (f32[12,64]{1,0:T(8,128)S(1)}, f32[12,64]{1,0:T(8,128)}, u32[]{:S(2)}) copy-start(f32[12,64]{1,0:T(8,128)} %param.34) | copy-start | bytes 9220
  158.1 2.5 %copy-start.40 = (f32[12,64]{1,0:T(8,128)S(1)}, f32[12,64]{1,0:T(8,128)}, u32[]{:S(2)}) copy-start(f32[12,64]{1,0:T(8,128)} %param.35) | copy-start | bytes 9220
  (19 other events, 25.4 us)
